TPU v7x, 32 devices: a whole 2x2x4 slice. The times are simulated.
32 devices in a mesh: bel: 8 (over z, x), st: 4 (over y, core).
Axes of the slice: x: 2, y: 2, z: 4, core: 2. Of those that a mesh axis runs over, the one named last changes fastest.
Arguments:
- alphas: bfloat16 [512, 12288], P(None, 'st'), may hold values from -120 to 120
- transitions: bfloat16 [6, 12288, 12288], P(None, 'bel', 'st'), may hold values from 0.0009994507 to 10
- observe: bfloat16 [6, 48, 12288], P(None, None, 'st'), may hold values from 0.0019989014 to 0.19921875
- reward: bfloat16 [6, 12288], P(None, 'bel'), may hold values from -1.796875 to 1.796875
- belief_index: int32 [128, 6, 48], P('bel'), may hold values from 0 to 511
- action: int32 [128], replicated, may hold values from 0 to 5
Outputs:
- new_alphas: bfloat16 [128, 12288], P('st', 'bel')
Inputs may be any that keep to these rules, and one draw needn't show every extreme that they name: `belief_index`: indices of rows of alphas.
All inputs are finite; a program needn't handle non-finite values.
Results may differ from a plain program's by a relative error of at most 0.0044.
Values may be sent and summed in bfloat16 or wider, within the bound.
A program may use at most 128 MiB of HBM per device.

v0:
```python
import math

import jax
import jax.numpy as jnp
from jax import lax
from jax.sharding import PartitionSpec as P

S = 12288
ACTS = 6


discount = 0.95


def mixture_block(alphas, observe, index_rows, action_rows):
    onehot = action_rows[:, None] == jnp.arange(ACTS, dtype=jnp.int32)[None, :]
    chosen = jnp.sum(jnp.where(onehot[:, :, None], index_rows, 0), axis=1)
    picked = alphas[chosen]
    weights = observe[action_rows]
    mixed = jnp.einsum("bos,bos->bs", picked, weights, preferred_element_type=jnp.float32)
    return mixed.astype(jnp.bfloat16)


def grouped_product(rows, acts, weights, block):
    count = rows.shape[0]
    kinds = weights.shape[0]
    blocks = count // block + kinds - 1
    onehot = (acts[:, None] == jnp.arange(kinds, dtype=jnp.int32)[None, :]).astype(jnp.int32)
    totals = jnp.sum(onehot, axis=0)
    filled = (totals + block - 1) // block
    ends = jnp.cumsum(filled)
    starts = ends - filled
    before = jnp.cumsum(onehot, axis=0) - onehot
    rank = jnp.sum(before * onehot, axis=1)
    first = jnp.sum(onehot * starts[None, :], axis=1)
    target = first * block + rank
    source = (
        jnp.zeros((blocks * block,), jnp.int32).at[target].set(jnp.arange(count, dtype=jnp.int32))
    )
    padded = rows[source].reshape(blocks, block, rows.shape[1])
    owner = jnp.sum(
        (jnp.arange(blocks, dtype=jnp.int32)[:, None] >= ends[None, :]).astype(jnp.int32), axis=1
    )
    owner = jnp.minimum(owner, kinds - 1)

    def one_block(pair):
        part, which = pair
        matrix = lax.dynamic_index_in_dim(weights, which, 0, keepdims=False)
        return lax.dot_general(
            part, matrix, (((1,), (1,)), ((), ())), preferred_element_type=jnp.float32
        )

    result = lax.map(one_block, (padded, owner)).reshape(blocks * block, weights.shape[1])
    return result[target]


def body(alphas, transitions, observe, reward, belief_index, action):
    bel_rows = belief_index.shape[0]
    beliefs = action.shape[0]
    own_start = lax.axis_index("bel") * bel_rows
    own_action = lax.dynamic_slice_in_dim(action, own_start, bel_rows)
    mixture = mixture_block(alphas, observe, belief_index, own_action)
    gathered = lax.all_gather(mixture, "bel", axis=0, tiled=True)
    terms = grouped_product(gathered, action, transitions, math.gcd(beliefs, 256))
    summed = lax.psum_scatter(terms, "st", scatter_dimension=0, tiled=True)
    out_rows = summed.shape[0]
    row_action = lax.dynamic_slice_in_dim(action, lax.axis_index("st") * out_rows, out_rows)
    onehot = (row_action[:, None] == jnp.arange(ACTS, dtype=jnp.int32)[None, :]).astype(
        jnp.bfloat16
    )
    gained = jnp.dot(onehot, reward, preferred_element_type=jnp.float32)
    return (gained + discount / S * summed).astype(jnp.bfloat16)


def solution(mesh):
    placed = (
        P(None, "st"),
        P(None, "bel", "st"),
        P(None, None, "st"),
        P(None, "bel"),
        P("bel", None, None),
        P(),
    )
    return jax.shard_map(
        body, mesh=mesh, in_specs=placed, out_specs=P("st", "bel"), check_vma=False
    )
```

profile of v0, /device:TPU:0, one launch (start us, length us, event | category | flops | bytes accessed | tf_op | source)
XLA Modules:
  0.0 167.2 jit_solution(12514179702635672855)
XLA Ops:
  6.5 0.0 copy-start
  6.5 0.0 reduce-scatter.2.cloned.1.call-start
  6.5 0.9 fusion.15
  7.4 0.8 fusion.14
  8.3 0.7 compare_select_fusion.3
  9.0 0.9 select_reduce_fusion.2
  9.9 0.1 reshape.164
  10.0 0.0 copy-done
  10.0 5.0 %gather_fusion = bf16[768,3072]{1,0:T(8,128)(2,1)} fusion(bf16[512,3072]{1,0:T(8,128)(2,1)S(1)} %copy-done, s32[1024]{0:T(1024)S(1)} %pad_clamp_fusion.3), kind=kCustom, calls=%fused_computation | custom fusion | bytes 9440256 | tf_op jit(solution)/shard_map/gather | solution.py:18
  15.0 4.6 %gather_fusion.1 = bf16[16,48,3072]{2,1,0:T(8,128)(2,1)} fusion(bf16[6,48,3072]{2,1,0:T(8,128)(2,1)} %param.10, s32[1024]{0:T(1024)S(1)} %pad_clamp_fusion.2), kind=kCustom, calls=%fused_computation.1 | custom fusion | bytes 9437248 | tf_op jit(solution)/shard_map/gather | solution.py:19
  19.5 0.0 copy-start.3
  19.5 5.7 %fusion.12 = bf16[16,3072]{1,0:T(8,128)(2,1)S(1)} fusion(bf16[16,3072,48]{1,2,0:T(8,128)(2,1)} %bitcast.49, bf16[16,48,3072]{2,1,0:T(8,128)(2,1)} %gather_fusion.1), kind=kLoop, calls=%fused_computation.14 | loop fusion | flops 9388032 | bytes 9535488 | tf_op jit(solution)/shard_map/bos,bos->bs/dot_general | solution.py:20
  25.3 33.9 %all_gather.3 = bf16[128,3072]{1,0:T(8,128)(2,1)S(1)} all-gather(bf16[16,3072]{1,0:T(8,128)(2,1)S(1)} %fusion.12), channel_id=1, replica_groups=mesh['bel'=8,'st'=4] {'bel'}, dimensions={0}, use_global_device_ids=true | all-gather | bytes 884736 | tf_op jit(solution)/shard_map/all_gather | solution.py:63
  59.2 0.2 reduce-window.7
  59.4 0.2 reduce_window_sum.18
  59.5 0.0 copy-done.3
  59.5 0.2 select_reduce_fusion.1
  59.8 1.0 scatter_custom_fusion
  60.8 0.1 convert_reduce_fusion
  60.9 5.0 %gather_fusion.2 = bf16[768,3072]{1,0:T(8,128)(2,1)} fusion(bf16[128,3072]{1,0:T(8,128)(2,1)S(1)} %all_gather.3, s32[1024]{0:T(1024)S(1)} %pad_clamp_fusion.1), kind=kCustom, calls=%fused_computation.2 | custom fusion | bytes 9440256 | tf_op jit(solution)/shard_map/gather | solution.py:40
  65.9 63.7 %while.10 = (s32[]{:T(128)}, f32[6,128,1536]{2,1,0:T(8,128)}, bf16[6,128,3072]{2,1,0:T(8,128)(2,1)}, s32[6]{0:T(128)S(1)}, bf16[6,1536,3072]{2,1,0:T(8,128)(2,1)}, /*index=5*/s32[]{:T(128)}, s32[]{:T(128)}, s32[]{:T(128)}) while((s32[]{:T(128)}, f32[6,128,1536]{2,1,0:T(8,128)}, bf16[6,128,3072]{2,1,0:T(8,128)(2,1)}, s32[6]{0:T(128)S(1)}, ...), condition=%wide.region_9.10_spmd, body=%wide.region_8.9_spmd.sunk | while | flops 1207959552 | bytes 11011207 | solution.py:53
  65.9 0.6 dynamic_slice.38
  68.4 8.1 %fusion.27 = f32[6,128,1536]{2,1,0:T(8,128)} fusion(f32[6,128,1536]{2,1,0:T(8,128)} %get-tuple-element.87, s32[]{:T(128)} %get-tuple-element.86, bf16[6,1536,3072]{2,1,0:T(8,128)(2,1)} %get-tuple-element.98, s32[]{:T(128)S(6)} %select_n.80, bf16[6,128,3072]{2,1,0:T(8,128)(2,1)} %get-tuple-element.96), kind=kOutput, calls=%fused_computation.9.clone.1 | convolution fusion | flops 1207959552 | bytes 11011076 | tf_op jit(solution)/shard_map/while/body/eval_jaxpr/dot_general | solution.py:49
  76.5 0.6 dynamic_slice.38
  79.0 8.1 %fusion.27 = f32[6,128,1536]{2,1,0:T(8,128)} fusion(f32[6,128,1536]{2,1,0:T(8,128)} %get-tuple-element.87, s32[]{:T(128)} %get-tuple-element.86, bf16[6,1536,3072]{2,1,0:T(8,128)(2,1)} %get-tuple-element.98, s32[]{:T(128)S(6)} %select_n.80, bf16[6,128,3072]{2,1,0:T(8,128)(2,1)} %get-tuple-element.96), kind=kOutput, calls=%fused_computation.9.clone.1 | convolution fusion | flops 1207959552 | bytes 11011076 | tf_op jit(solution)/shard_map/while/body/eval_jaxpr/dot_general | solution.py:49
  87.1 0.6 dynamic_slice.38
  89.6 8.1 %fusion.27 = f32[6,128,1536]{2,1,0:T(8,128)} fusion(f32[6,128,1536]{2,1,0:T(8,128)} %get-tuple-element.87, s32[]{:T(128)} %get-tuple-element.86, bf16[6,1536,3072]{2,1,0:T(8,128)(2,1)} %get-tuple-element.98, s32[]{:T(128)S(6)} %select_n.80, bf16[6,128,3072]{2,1,0:T(8,128)(2,1)} %get-tuple-element.96), kind=kOutput, calls=%fused_computation.9.clone.1 | convolution fusion | flops 1207959552 | bytes 11011076 | tf_op jit(solution)/shard_map/while/body/eval_jaxpr/dot_general | solution.py:49
  97.7 0.6 dynamic_slice.38
  100.2 8.1 %fusion.27 = f32[6,128,1536]{2,1,0:T(8,128)} fusion(f32[6,128,1536]{2,1,0:T(8,128)} %get-tuple-element.87, s32[]{:T(128)} %get-tuple-element.86, bf16[6,1536,3072]{2,1,0:T(8,128)(2,1)} %get-tuple-element.98, s32[]{:T(128)S(6)} %select_n.80, bf16[6,128,3072]{2,1,0:T(8,128)(2,1)} %get-tuple-element.96), kind=kOutput, calls=%fused_computation.9.clone.1 | convolution fusion | flops 1207959552 | bytes 11011076 | tf_op jit(solution)/shard_map/while/body/eval_jaxpr/dot_general | solution.py:49
  108.3 0.6 dynamic_slice.38
  110.8 8.1 %fusion.27 = f32[6,128,1536]{2,1,0:T(8,128)} fusion(f32[6,128,1536]{2,1,0:T(8,128)} %get-tuple-element.87, s32[]{:T(128)} %get-tuple-element.86, bf16[6,1536,3072]{2,1,0:T(8,128)(2,1)} %get-tuple-element.98, s32[]{:T(128)S(6)} %select_n.80, bf16[6,128,3072]{2,1,0:T(8,128)(2,1)} %get-tuple-element.96), kind=kOutput, calls=%fused_computation.9.clone.1 | convolution fusion | flops 1207959552 | bytes 11011076 | tf_op jit(solution)/shard_map/while/body/eval_jaxpr/dot_general | solution.py:49
  118.9 0.6 dynamic_slice.38
  121.4 8.2 %fusion.27 = f32[6,128,1536]{2,1,0:T(8,128)} fusion(f32[6,128,1536]{2,1,0:T(8,128)} %get-tuple-element.87, s32[]{:T(128)} %get-tuple-element.86, bf16[6,1536,3072]{2,1,0:T(8,128)(2,1)} %get-tuple-element.98, s32[]{:T(128)S(6)} %select_n.80, bf16[6,128,3072]{2,1,0:T(8,128)(2,1)} %get-tuple-element.96), kind=kOutput, calls=%fused_computation.9.clone.1 | convolution fusion | flops 1207959552 | bytes 11011076 | tf_op jit(solution)/shard_map/while/body/eval_jaxpr/dot_general | solution.py:49
  129.6 0.0 copy-start.2
  129.6 0.0 copy-start.1
  129.6 4.6 %gather_fusion.3 = f32[128,1536]{1,0:T(8,128)} fusion(f32[768,1536]{1,0:T(8,128)} %bitcast.51, s32[1024]{0:T(1024)S(1)} %pad_clamp_fusion), kind=kCustom, calls=%fused_computation.3 | custom fusion | bytes 1573376 | tf_op jit(solution)/shard_map/gather | solution.py:54
  134.2 0.0 reduce-scatter.2.cloned.1.call-update
  134.2 0.1 dynamic_slice.18
  134.3 24.2 %reduce-scatter.2.cloned.1.call-done = f32[32,1536]{1,0:T(8,128)} async-done(((f32[128,1536]{1,0:T(8,128)}), f32[32,1536]{1,0:T(8,128)}) %reduce-scatter.2.cloned.1.call-update) | async-done | bytes 196624 | tf_op jit(solution)/shard_map/reduce_scatter | solution.py:65
  158.5 0.0 copy-done.2
  158.5 1.8 %fusion.13 = bf16[32,1536]{1,0:T(8,128)(2,1)} fusion(bf16[6,1536]{1,0:T(8,128)(2,1)S(1)} %copy-done.2, f32[32,1536]{1,0:T(8,128)} %reduce-scatter.2.cloned.1.call-done, s32[32]{0:T(128)S(1)} %dynamic_slice.18), kind=kOutput, calls=%fused_computation.16 | convolution fusion | flops 737472 | bytes 313472 | tf_op jit(solution)/shard_map/dot_general | solution.py:71
  160.3 0.0 copy-done.1
  (13 shorter events, 0.1 us)
Async XLA Ops:
  6.5 3.5 %copy-start = (bf16[512,3072]{1,0:T(8,128)(2,1)S(1)}, bf16[512,3072]{1,0:T(8,128)(2,1)}, u32[]{:S(2)}) copy-start(bf16[512,3072]{1,0:T(8,128)(2,1)} %param.8) | copy-start | bytes 9437188
  6.5 152.0 %reduce-scatter.2.cloned.1.call-start = ((), (), s32[]{:S(2)}) async-start(), calls=%async_computation.1 | async-start | bytes 983040 | tf_op jit(solution)/shard_map/reduce_scatter | solution.py:65
  19.5 40.0 %copy-start.3 = (s32[128]{0:T(128)S(1)}, s32[128]{0:T(128)}, u32[]{:S(2)}) copy-start(s32[128]{0:T(128)} %param.13) | copy-start | bytes 1540
  129.6 28.9 %copy-start.2 = (bf16[6,1536]{1,0:T(8,128)(2,1)S(1)}, bf16[6,1536]{1,0:T(8,128)(2,1)}, u32[]{:S(2)}) copy-start(bf16[6,1536]{1,0:T(8,128)(2,1)} %param.11) | copy-start | bytes 55300
  129.6 30.7 %copy-start.1 = (bf16[512,3072]{1,0:T(8,128)(2,1)S(1)}, bf16[512,3072]{1,0:T(8,128)(2,1)}, u32[]{:S(2)}) copy-start(bf16[512,3072]{1,0:T(8,128)(2,1)} %param.8) | copy-start | bytes 9437188
Sparse Core Ops, SparseCore 0:
  134.3 24.1 reduce-scatter.1
where the time goes:
time: 168 us; the launch traced here: 167 us
  matrix products  50.4 us (30%)
  blocking collectives  33.9 us (20%)
  waiting for transfers between devices  24.2 us (14%)
  local copies, waits for them, and re-layouts  24 us (14%)
  between operations  13.5 us (8%)
  loops' own time  11.3 us (7%)
  other arithmetic  9.78 us (6%)
    dot_general x6, matrix products, one_block(): lax.dot_general(part, matrix, (((1,), (1,)), ((), ())), preferred_element...  48.6 us
    all_gather x1, blocking collectives, body(): gathered = lax.all_gather(mixture, 'bel', axis=0, tiled=True)  33.9 us
    reduce_scatter x1, waiting for transfers between devices, body(): summed = lax.psum_scatter(terms, 'st', scatter_dimension=0, tiled=True)  24.2 us
    another operation x1, loops' own time, grouped_product(): lax.map(one_block, (padded, owner))  11.3 us
    dot_general x1, other arithmetic, mixture_block(): jnp.einsum('bos,bos->bs', picked, weights, preferred_element_type=jnp.flo...  5.75 us
    gather x1, local copies, waits for them, and re-layouts, mixture_block(): picked = alphas[chosen]  4.96 us
    gather x1, local copies, waits for them, and re-layouts, grouped_product(): padded = rows[source].reshape(blocks, block, rows.shape[1])  4.95 us
    gather x1, local copies, waits for them, and re-layouts, grouped_product(): return result[target]  4.6 us
  transfers between devices with their start and end apart: 1, of which 1 were waited for; matrix products, arithmetic and copies ran while one was open for 0% of the time, Pallas kernels for 0%

commit v1 on v0

v1 whole, which is shorter than its diff:
```python
import functools
import math

import jax
import jax.numpy as jnp
from jax import lax
from jax.experimental import pallas as pl
from jax.experimental.pallas import tpu as pltpu
from jax.sharding import PartitionSpec as P

discount = 0.95
MESH = pl.DeviceIdType.MESH
VMEM_BYTES = 67_043_328


def kernel(
    n_bel,
    n_st,
    scale,
    act_s,
    act_row,
    bi,
    reward,
    alphas_h,
    obs_h,
    w_h,
    out,
    alphas_v,
    obs_v,
    w_v,
    onehot,
    act_col,
    mixf,
    mix,
    terms,
    recv,
    in_sem,
    w_sem,
    ag_send,
    ag_recv,
    rs_send,
    rs_recv,
):
    own, acts, obs = bi.shape
    k_rows = alphas_v.shape[0]
    beliefs, depth = mix.shape
    nj, _, nb, _ = w_v.shape
    out_rows = out.shape[0]
    n_chunk = ag_send.shape[1]
    width = depth // n_chunk
    block = act_row.shape[1]
    half = n_bel // 2

    load_alphas = pltpu.make_async_copy(alphas_h, alphas_v, in_sem.at[0])
    load_obs = pltpu.make_async_copy(obs_h, obs_v, in_sem.at[1])
    load_alphas.start()
    load_obs.start()

    def load_w(j, a):
        return pltpu.make_async_copy(
            w_h.at[a, pl.ds(j * nb, nb), :], w_v.at[j, a], w_sem.at[j, a]
        )

    for j in range(nj):
        for a in range(acts):
            load_w(j, a).start()

    me = lax.axis_index("bel")
    st = lax.axis_index("st")
    odd = lax.rem(me, 2)
    pos = (1 - odd) * (me // 2) + odd * (n_bel - 1 - me // 2)

    def at_pos(p):
        p = lax.rem(p + n_bel, n_bel)
        back = p // half
        return (1 - back) * (2 * p) + back * (2 * (n_bel - 1 - p) + 1)

    right, left = at_pos(pos + 1), at_pos(pos - 1)

    barrier = pltpu.get_barrier_semaphore()
    for neighbour in (right, left):
        pl.semaphore_signal(barrier, inc=1, device_id={"bel": neighbour}, device_id_type=MESH)
    for d in range(1, n_st):
        pl.semaphore_signal(
            barrier, inc=1, device_id={"st": lax.rem(st + d, n_st)}, device_id_type=MESH
        )

    eye = lax.broadcasted_iota(jnp.int32, (block, block), 0) == lax.broadcasted_iota(
        jnp.int32, (block, block), 1
    )
    for r in range(beliefs // block):
        row = act_row[r : r + 1, :].astype(jnp.float32)
        act_col[r * block : (r + 1) * block, :] = jnp.sum(
            jnp.where(eye, row, 0.0), axis=1, keepdims=True
        )
    eye_o = lax.broadcasted_iota(jnp.int32, (obs, obs), 0) == lax.broadcasted_iota(
        jnp.int32, (obs, obs), 1
    )
    lanes = lax.broadcasted_iota(jnp.int32, (obs, k_rows), 1).astype(jnp.float32)
    for i in range(own):
        a = act_s[me * own + i]
        row = bi[i, pl.ds(a, 1), :].astype(jnp.float32)
        col = jnp.sum(jnp.where(eye_o, row, 0.0), axis=1, keepdims=True)
        onehot[i * obs : (i + 1) * obs, :] = jnp.where(lanes == col, 1.0, 0.0).astype(jnp.bfloat16)

    load_alphas.wait()
    load_obs.wait()
    pl.semaphore_wait(barrier, 2 + n_st - 1)

    def shard(src, c):
        return mix.at[
            pl.ds(pl.multiple_of(src * own, own), own), pl.ds(c * width, width)
        ]

    def send(direction, c, hop, src):
        piece = shard(src, c)
        return pltpu.make_async_remote_copy(
            src_ref=piece,
            dst_ref=piece,
            send_sem=ag_send.at[direction, c, hop],
            recv_sem=ag_recv.at[direction, c, hop],
            device_id={"bel": right if direction == 0 else left},
            device_id_type=MESH,
        )

    def hops(direction, c):
        return half if (direction + c) % 2 == 0 else n_bel - 1 - half

    group = math.gcd(own, 4)
    for c in range(n_chunk):
        cols = slice(c * width, (c + 1) * width)

        def one_group(g, carry, cols=cols):
            first = pl.multiple_of(g * (group * obs), group * obs)
            picked = jnp.dot(
                onehot[pl.ds(first, group * obs), :],
                alphas_v[:, cols],
                preferred_element_type=jnp.float32,
            )
            for i in range(group):
                a = act_s[me * own + g * group + i]
                weights = obs_v[a, :, cols].astype(jnp.float32)
                part = picked[i * obs : (i + 1) * obs, :] * weights
                mixf[pl.ds(g * group + i, 1), cols] = jnp.sum(part, axis=0, keepdims=True)
            return carry

        lax.fori_loop(0, own // group, one_group, 0)
        mix[pl.ds(pl.multiple_of(me * own, own), own), cols] = mixf[:, cols].astype(jnp.bfloat16)
        for direction in range(2):
            if hops(direction, c) > 0:
                send(direction, c, 0, me).start()

    most = max(half, n_bel - 1 - half)

    def source(direction, hop):
        return at_pos(pos - 1 - hop) if direction == 0 else at_pos(pos + 1 + hop)

    for hop in range(most):
        for c in range(n_chunk):
            for direction in range(2):
                total = hops(direction, c)
                if hop < total:
                    src = source(direction, hop)
                    send(direction, c, hop, src).wait_recv()
                    if hop + 1 < total:
                        send(direction, c, hop + 1, src).start()

    def rs_copy(j, d):
        peer = lax.rem(st + d, n_st)
        return pltpu.make_async_remote_copy(
            src_ref=terms.at[j, pl.ds(pl.multiple_of(peer * out_rows, out_rows), out_rows), :],
            dst_ref=recv.at[d - 1, j],
            send_sem=rs_send.at[j, d - 1],
            recv_sem=rs_recv.at[j, d - 1],
            device_id={"st": peer},
            device_id_type=MESH,
        )

    def one_column_block(j, carry):
        for a in range(acts):
            load_w(j, a).wait()
        for r in range(beliefs // block):
            rows = slice(r * block, (r + 1) * block)
            which = act_col[rows, :]
            total = jnp.zeros((block, nb), jnp.float32)
            for a in range(acts):
                keep = jnp.where(which == float(a), 1.0, 0.0).astype(jnp.bfloat16)
                total += lax.dot_general(
                    mix[rows, :] * keep,
                    w_v[j, a],
                    (((1,), (1,)), ((), ())),
                    preferred_element_type=jnp.float32,
                )
            terms[j, rows, :] = total
        for d in range(1, n_st):
            rs_copy(j, d).start()
        return carry

    lax.fori_loop(0, nj, one_column_block, 0)

    mine = pl.ds(pl.multiple_of(st * out_rows, out_rows), out_rows)
    which = act_col[mine, :]
    for j in range(nj):
        cols = slice(j * nb, (j + 1) * nb)
        gained = jnp.zeros((out_rows, nb), jnp.float32)
        for a in range(acts):
            gained += jnp.where(
                which == float(a), reward[a : a + 1, cols].astype(jnp.float32), 0.0
            )
        total = terms[j, mine, :]
        for d in range(1, n_st):
            rs_copy(j, d).wait_recv()
            total += recv[d - 1, j]
        out[:, cols] = (gained + scale * total).astype(out.dtype)

    for j in range(nj):
        for d in range(1, n_st):
            rs_copy(j, d).wait_send()
    for direction in range(2):
        for c in range(n_chunk):
            for hop in range(hops(direction, c)):
                src = me if hop == 0 else source(direction, hop - 1)
                send(direction, c, hop, src).wait_send()


def body(n_bel, n_st, alphas, transitions, observe, reward, belief_index, action):
    k_rows, depth = alphas.shape
    acts, states, _ = transitions.shape
    obs = observe.shape[1]
    own = belief_index.shape[0]
    beliefs = action.shape[0]
    out_rows = beliefs // n_st
    block = math.gcd(beliefs, 128)
    nb = 256 if states % 256 == 0 else states
    nj = states // nb
    n_chunk = 4 if n_bel <= 16 else 1
    most = max(n_bel // 2, 1)
    scale = discount / (depth * n_st)
    vmem = pl.BlockSpec(memory_space=pltpu.VMEM)
    hbm = pl.BlockSpec(memory_space=pl.ANY)
    return pl.pallas_call(
        functools.partial(kernel, n_bel, n_st, scale),
        out_shape=jax.ShapeDtypeStruct((out_rows, states), jnp.bfloat16),
        in_specs=[pl.BlockSpec(memory_space=pltpu.SMEM), vmem, vmem, vmem, hbm, hbm, hbm],
        out_specs=vmem,
        scratch_shapes=[
            pltpu.VMEM((k_rows, depth), jnp.bfloat16),
            pltpu.VMEM((acts, obs, depth), jnp.bfloat16),
            pltpu.VMEM((nj, acts, nb, depth), jnp.bfloat16),
            pltpu.VMEM((own * obs, k_rows), jnp.bfloat16),
            pltpu.VMEM((beliefs, 1), jnp.float32),
            pltpu.VMEM((own, depth), jnp.float32),
            pltpu.VMEM((beliefs, depth), jnp.bfloat16),
            pltpu.VMEM((nj, beliefs, nb), jnp.float32),
            pltpu.VMEM((n_st - 1, nj, out_rows, nb), jnp.float32),
            pltpu.SemaphoreType.DMA((2,)),
            pltpu.SemaphoreType.DMA((nj, acts)),
            pltpu.SemaphoreType.DMA((2, n_chunk, most)),
            pltpu.SemaphoreType.DMA((2, n_chunk, most)),
            pltpu.SemaphoreType.DMA((nj, n_st - 1)),
            pltpu.SemaphoreType.DMA((nj, n_st - 1)),
        ],
        compiler_params=pltpu.CompilerParams(
            collective_id=0, has_side_effects=True, vmem_limit_bytes=VMEM_BYTES
        ),
    )(
        action,
        action.reshape(beliefs // block, block),
        belief_index,
        reward,
        alphas,
        observe,
        transitions,
    )


def solution(mesh):
    placed = (
        P(None, "st"),
        P(None, "bel", "st"),
        P(None, None, "st"),
        P(None, "bel"),
        P("bel", None, None),
        P(),
    )
    return jax.shard_map(
        functools.partial(body, mesh.shape["bel"], mesh.shape["st"]),
        mesh=mesh,
        in_specs=placed,
        out_specs=P("st", "bel"),
        check_vma=False,
    )
```

time: 168 us -> 67.6 us (0.40)
  Pallas kernels: 0 us -> 64.4 us
  matrix products: 50.4 us -> 0 us
  blocking collectives: 33.9 us -> 0 us
  waiting for transfers between devices: 24.2 us -> 0 us
  local copies, waits for them, and re-layouts: 24 us -> 2.99 us
  between operations: 13.5 us -> 0.01 us
  loops' own time: 11.3 us -> 0 us
  other arithmetic: 9.78 us -> 0 us
    pallas_call x0 -> x1, Pallas kernels: none -> 64.4 us  [body(): pl.pallas_call(functools.partial(kernel, n_bel, n_st, scale), out_shape=j...]
    dot_general x7 -> x0, matrix products: 50.4 us -> none  [the longest x6 48.6 us: one_block(): lax.dot_general(part, matrix, (((1,), (1,)), ((), ())), preferred_element...]
    all_gather x1 -> x0, blocking collectives: 33.9 us -> none  [body(): gathered = lax.all_gather(mixture, 'bel', axis=0, tiled=True)]
    reduce_scatter x1 -> x0, waiting for transfers between devices: 24.2 us -> none  [body(): summed = lax.psum_scatter(terms, 'st', scatter_dimension=0, tiled=True)]
    gather x4 -> x0, local copies, waits for them, and re-layouts: 19.1 us -> none  [the longest x1 4.96 us: mixture_block(): picked = alphas[chosen]]
    another operation x1 -> x0, loops' own time: 11.3 us -> none  [grouped_product(): lax.map(one_block, (padded, owner))]
    dot_general x1 -> x0, other arithmetic: 5.75 us -> none  [mixture_block(): jnp.einsum('bos,bos->bs', picked, weights, preferred_element_type=jnp.flo...]
    dynamic_slice x7 -> x0, local copies, waits for them, and re-layouts: 3.87 us -> none  [the longest x6 3.8 us: grouped_product(): lax.map(one_block, (padded, owner))]
  transfers between devices with their start and end apart: 1 -> 0, of which waited for: 1 -> 0; matrix products, arithmetic and copies ran while one was open for 0% -> 0% of each run, Pallas kernels for 0% -> 0%
where the time goes in v1:
time: 67.6 us; the launch traced here: 67.4 us
  Pallas kernels  64.4 us (95%)
  local copies, waits for them, and re-layouts  2.99 us (4%)
    pallas_call x1, Pallas kernels, body(): pl.pallas_call(functools.partial(kernel, n_bel, n_st, scale), out_shape=j...  64.4 us
    unnamed x2, local copies, waits for them, and re-layouts  2.99 us

profile of v1, /device:TPU:0, one launch (start us, length us, event | category | flops | bytes accessed | tf_op | source)
XLA Modules:
  0.0 67.4 jit_solution(8753069108082692246)
XLA Ops:
  0.0 1.4 %copy.7.bi = s32[16,6,48]{2,1,0:T(8,128)} copy(s32[16,6,48]{2,0,1:T(8,128)} %param.10) | data formatting | bytes 36864 | tf_op args[4]
  1.4 64.4 %shard_map.64 = bf16[32,1536]{1,0:T(8,128)(2,1)} custom-call(s32[128]{0:T(128)} %act_s.1, s32[1,128]{1,0:T(1,128)} %bitcast.1, s32[16,6,48]{2,1,0:T(8,128)} %copy.7.bi, bf16[6,1536]{1,0:T(8,128)(2,1)} %reward.1, bf16[512,3072]{1,0:T(8,128)(2,1)} %alphas_h.1, bf16[6,48,3072]{2,1,0:T(8,128)(2,1)} %obs_h.1, bf16[6,1536,3072]{2,1,0:T(8,128)(2,1)} %w_h.1), custom_call_target="tpu_custom_call" | custom-call | tf_op jit(solution)/shard_map/pallas_call | solution.py:241
  65.9 1.5 %copy.9 = bf16[32,1536]{1,0:T(8,128)(2,1)} copy(bf16[32,1536]{1,0:T(8,128)(2,1)} %shard_map.64) | data formatting | bytes 196608

commit v2 on v1

--- a/solution.py
+++ b/solution.py
@@ -61,10 +61,6 @@
             w_h.at[a, pl.ds(j * nb, nb), :], w_v.at[j, a], w_sem.at[j, a]
         )
 
-    for j in range(nj):
-        for a in range(acts):
-            load_w(j, a).start()
-
     me = lax.axis_index("bel")
     st = lax.axis_index("st")
     odd = lax.rem(me, 2)
@@ -105,6 +101,15 @@
 
     load_alphas.wait()
     load_obs.wait()
+    queue = list(range(nj))
+
+    def issue(count):
+        for j in queue[:count]:
+            for a in range(acts):
+                load_w(j, a).start()
+        del queue[:count]
+
+    issue((nj + 2) // 3)
     pl.semaphore_wait(barrier, 2 + n_st - 1)
 
     def shard(src, c):
@@ -127,10 +132,11 @@
         return half if (direction + c) % 2 == 0 else n_bel - 1 - half
 
     group = math.gcd(own, 4)
-    for c in range(n_chunk):
+
+    def mixture(c):
         cols = slice(c * width, (c + 1) * width)
 
-        def one_group(g, carry, cols=cols):
+        def one_group(g, carry):
             first = pl.multiple_of(g * (group * obs), group * obs)
             picked = jnp.dot(
                 onehot[pl.ds(first, group * obs), :],
@@ -146,17 +152,21 @@
 
         lax.fori_loop(0, own // group, one_group, 0)
         mix[pl.ds(pl.multiple_of(me * own, own), own), cols] = mixf[:, cols].astype(jnp.bfloat16)
-        for direction in range(2):
-            if hops(direction, c) > 0:
-                send(direction, c, 0, me).start()
 
     most = max(half, n_bel - 1 - half)
 
     def source(direction, hop):
         return at_pos(pos - 1 - hop) if direction == 0 else at_pos(pos + 1 + hop)
 
-    for hop in range(most):
-        for c in range(n_chunk):
+    for step in range(n_chunk + most):
+        if step < n_chunk:
+            mixture(step)
+            for direction in range(2):
+                if hops(direction, step) > 0:
+                    send(direction, step, 0, me).start()
+        issue(1 if step < n_chunk - 1 else nj)
+        for c in range(min(step, n_chunk)):
+            hop = step - 1 - c
             for direction in range(2):
                 total = hops(direction, c)
                 if hop < total:
@@ -182,16 +192,16 @@
         for r in range(beliefs // block):
             rows = slice(r * block, (r + 1) * block)
             which = act_col[rows, :]
-            total = jnp.zeros((block, nb), jnp.float32)
+            total = jnp.zeros((nb, block), jnp.float32)
             for a in range(acts):
                 keep = jnp.where(which == float(a), 1.0, 0.0).astype(jnp.bfloat16)
                 total += lax.dot_general(
+                    w_v[j, a],
                     mix[rows, :] * keep,
-                    w_v[j, a],
                     (((1,), (1,)), ((), ())),
                     preferred_element_type=jnp.float32,
                 )
-            terms[j, rows, :] = total
+            terms[j, rows, :] = total.T
         for d in range(1, n_st):
             rs_copy(j, d).start()
         return carry
@@ -231,7 +241,7 @@
     beliefs = action.shape[0]
     out_rows = beliefs // n_st
     block = math.gcd(beliefs, 128)
-    nb = 256 if states % 256 == 0 else states
+    nb = 512 if states % 512 == 0 else states
     nj = states // nb
     n_chunk = 4 if n_bel <= 16 else 1
     most = max(n_bel // 2, 1)

time: 67.6 us -> 53.4 us (0.79)
  Pallas kernels: 64.4 us -> 50.1 us
    pallas_call x1, Pallas kernels: 64.4 us -> 50.1 us  [body(): pl.pallas_call(functools.partial(kernel, n_bel, n_st, scale), out_shape=j...]
where the time goes in v2:
time: 53.4 us; the launch traced here: 53.1 us
  Pallas kernels  50.1 us (94%)
  local copies, waits for them, and re-layouts  2.99 us (6%)
    pallas_call x1, Pallas kernels, body(): pl.pallas_call(functools.partial(kernel, n_bel, n_st, scale), out_shape=j...  50.1 us
    unnamed x2, local copies, waits for them, and re-layouts  2.99 us

profile of v2, /device:TPU:0, one launch (start us, length us, event | category | flops | bytes accessed | tf_op | source)
XLA Modules:
  0.0 53.1 jit_solution(7800210243862831323)
XLA Ops:
  0.0 1.4 %copy.7.bi = s32[16,6,48]{2,1,0:T(8,128)} copy(s32[16,6,48]{2,0,1:T(8,128)} %param.10) | data formatting | bytes 36864 | tf_op args[4]
  1.4 50.1 %shard_map.64 = bf16[32,1536]{1,0:T(8,128)(2,1)} custom-call(s32[128]{0:T(128)} %act_s.1, s32[1,128]{1,0:T(1,128)} %bitcast.1, s32[16,6,48]{2,1,0:T(8,128)} %copy.7.bi, bf16[6,1536]{1,0:T(8,128)(2,1)} %reward.1, bf16[512,3072]{1,0:T(8,128)(2,1)} %alphas_h.1, bf16[6,48,3072]{2,1,0:T(8,128)(2,1)} %obs_h.1, bf16[6,1536,3072]{2,1,0:T(8,128)(2,1)} %w_h.1), custom_call_target="tpu_custom_call" | custom-call | tf_op jit(solution)/shard_map/pallas_call | solution.py:251
  51.6 1.5 %copy.9 = bf16[32,1536]{1,0:T(8,128)(2,1)} copy(bf16[32,1536]{1,0:T(8,128)(2,1)} %shard_map.64) | data formatting | bytes 196608
